TPU v7x, 256 devices: a whole 4x4x8 slice. The times are simulated.
256 devices in a mesh: dp: 16 (over z_hi, y), fsdp: 16 (over x, z_lo, core).
Axes of the slice: x: 4, y: 4, z: 8 (z_hi: 4, z_lo: 2; z = z_hi * 2 + z_lo), core: 2. Of those that a mesh axis runs over, the one named last changes fastest.
Arguments:
- features: bfloat16 [49152, 8192], P(('dp', 'fsdp')), may hold values from -6 to 6
- grad_out: bfloat16 [49152, 8192], P(('dp', 'fsdp')), may hold values from -6 to 6
- weight_tiles: bfloat16 [256, 128, 128], P('fsdp'), may hold values from -0.25 to 0.25
- tile_row: int32 [256], replicated, may hold values from 0 to 63, as said below
- tile_column: int32 [256], replicated, may hold values from 0 to 63, as said below
Outputs:
- grad_features: bfloat16 [49152, 8192], P(('dp', 'fsdp'))
- tile_update: float32 [256, 128, 128], P('fsdp')
Inputs may be any that keep to these rules, and one draw needn't show every extreme that they name: `tile_row`: every tile-row holds exactly 4 stored tiles; the tile-columns of tile-row i are i XOR s for the four values s in (0, 2^a, 2^b, 2^a + 2^b), with two distinct bits a, b drawn per run; the stored order is a random permutation of the pattern. Every tile-column holds exactly 4 stored tiles; no (tile_row, tile_column) pair appears twice.
All inputs are finite; a program needn't handle non-finite values.
Results may differ from a plain program's by a relative error of at most 0.0034.
Values may be sent and summed in bfloat16 or wider, within the bound.
No kernel may reach another device: no remote copies, remote signals or barrier semaphores. Data moves between devices by JAX's collectives and lax.ppermute only.
A program may use at most 128 MiB of HBM per device.

v0:
```python
import math
import jax
import jax.numpy as jnp
from jax import lax
from jax.sharding import PartitionSpec as P


def gelu_slope(value):
    root_term = math.sqrt(2.0 / math.pi)
    inner = root_term * (value + 0.044715 * value * value * value)
    hyper = jnp.tanh(inner)
    return 0.5 * (1.0 + hyper) + 0.5 * value * (1.0 - hyper * hyper) * root_term * (
        1.0 + 3.0 * 0.044715 * value * value
    )


def on_device(features, grad_out, weight_tiles, tile_row, tile_column):
    rows_here = features.shape[0]
    side = weight_tiles.shape[1]
    nblocks = features.shape[1] // side
    total_tiles = tile_row.shape[0]
    per_block = total_tiles // nblocks
    feature_blocks = features.reshape(rows_here, nblocks, side)
    grad_blocks = grad_out.reshape(rows_here, nblocks, side)
    order_rows = jnp.argsort(tile_row, stable=True)
    order_columns = jnp.argsort(tile_column, stable=True)
    columns_by_row = tile_column[order_rows].reshape(nblocks, per_block)
    rows_by_column = tile_row[order_columns].reshape(nblocks, per_block)
    whole = lax.all_gather(weight_tiles, "fsdp", axis=0, tiled=True)
    tiles_by_row = whole[order_rows].reshape(nblocks, per_block, side, side)
    taken = feature_blocks[:, columns_by_row]
    preact = jnp.einsum("rnkc,nkcd->rnd", taken, tiles_by_row, preferred_element_type=jnp.float32)
    slope_grad = (grad_blocks.astype(jnp.float32) * gelu_slope(preact)).astype(jnp.bfloat16)
    tiles_by_column = whole[order_columns].reshape(nblocks, per_block, side, side)
    slopes_taken = slope_grad[:, rows_by_column]
    returned = jnp.einsum(
        "rnkd,nkcd->rnc", slopes_taken, tiles_by_column, preferred_element_type=jnp.float32
    )
    grad_features = (
        (grad_blocks.astype(jnp.float32) + returned)
        .astype(jnp.bfloat16)
        .reshape(rows_here, nblocks * side)
    )
    tile_ids = jnp.arange(
        total_tiles // lax.axis_size("fsdp") * lax.axis_size("fsdp"), dtype=jnp.int32
    )
    columns = tile_column[tile_ids]
    row_ids = tile_row[tile_ids]
    picked = jnp.take(feature_blocks, columns, axis=1)
    slopes = jnp.take(slope_grad, row_ids, axis=1)
    summed = lax.psum_scatter(
        jnp.einsum("rnc,rnd->ncd", picked, slopes, preferred_element_type=jnp.float32),
        "fsdp",
        scatter_dimension=0,
        tiled=True,
    )
    weight_grad = lax.psum(summed, "dp")
    tile_update = weight_grad * lax.rsqrt(
        jnp.mean(weight_grad * weight_grad, axis=(1, 2), keepdims=True) + 1e-06
    )
    return (grad_features, tile_update)


def solution(mesh):
    return jax.shard_map(
        on_device,
        mesh=mesh,
        in_specs=(
            P(("dp", "fsdp"), None),
            P(("dp", "fsdp"), None),
            P("fsdp", None, None),
            P(),
            P(),
        ),
        out_specs=(P(("dp", "fsdp"), None), P("fsdp", None, None)),
        check_vma=False,
    )
```

profile of v0, /device:TPU:8, one launch (start us, length us, event | category | flops | bytes accessed | tf_op | source)
XLA Modules:
  0.0 482.4 jit_solution(4299826176216152528)
XLA Ops:
  7.2 0.0 copy-start
  7.2 0.0 all-gather.2.cloned.1.call-start
  7.2 0.7 all-gather.2.cloned.1.call-update
  7.9 0.0 reduce-scatter.2.cloned.1.call-start
  8.0 4.0 sort.32
  12.0 2.0 gather_fusion.7
  13.9 2.0 gather_fusion.6
  16.0 2.0 gather_fusion.2
  17.9 0.1 reshape.97
  18.1 0.1 reshape.143
  18.2 0.0 copy-done
  18.2 2.6 copy_bitcast_fusion.1
  20.7 0.0 copy-start.4
  20.7 12.8 %gather_fusion.3 = bf16[256,192,128]{2,1,0:T(8,128)(2,1)} fusion(bf16[192,64,128]{2,0,1:T(8,128)(2,1)} %copy_bitcast_fusion.1, s32[1024]{0:T(1024)S(1)} %pad_clamp_fusion.4), kind=kCustom, calls=%fused_computation.5 | custom fusion | bytes 25166848 | tf_op jit(solution)/shard_map/gather | solution.py:31
  33.6 0.0 copy-done.4
  33.6 10.8 %gather_fusion.8 = bf16[256,192,128]{2,1,0:T(8,128)(2,1)} fusion(bf16[192,64,128]{2,0,1:T(8,128)(2,1)S(1)} %copy-done.4, s32[1024]{0:T(1024)S(1)} %pad_clamp_fusion.1), kind=kCustom, calls=%fused_computation.clone | custom fusion | bytes 25166848 | tf_op jit(solution)/shard_map/jit(_take)/gather | solution.py:49
  44.4 23.1 %all-gather.2.cloned.1.call-done = bf16[256,128,128]{2,1,0:T(8,128)(2,1)} async-done(((bf16[16,128,128]{2,1,0:T(8,128)(2,1)}), bf16[256,128,128]{2,1,0:T(8,128)(2,1)}) %all-gather.2.cloned.1.call-update) | async-done | bytes 8388624 | tf_op jit(solution)/shard_map/all_gather | solution.py:29
  67.5 12.1 %gather_fusion.1 = bf16[256,128,128]{2,1,0:T(8,128)(2,1)} fusion(bf16[256,128,128]{2,1,0:T(8,128)(2,1)} %all-gather.2.cloned.1.call-done, s32[1024]{0:T(1024)S(1)} %pad_clamp_fusion.5), kind=kCustom, calls=%fused_computation.3 | custom fusion | bytes 16778240 | tf_op jit(solution)/shard_map/gather | solution.py:30
  79.6 11.0 %fusion.13 = bf16[192,64,128]{2,0,1:T(8,128)(2,1)S(1)} fusion(bf16[192,64,4,128]{3,0,2,1:T(8,128)(2,1)} %bitcast.65, bf16[64,4,128,128]{3,2,1,0:T(8,128)(2,1)} %bitcast.68, bf16[192,8192]{1,0:T(8,128)(2,1)} %param.8), kind=kOutput, calls=%fused_computation.25 | convolution fusion | flops 1642070016 | bytes 27262976 | tf_op jit(solution)/shard_map/rnkc,nkcd->rnd/dot_general | solution.py:32
  90.6 0.0 copy-start.5
  90.6 10.7 %gather_fusion.9 = bf16[256,192,128]{2,1,0:T(8,128)(2,1)} fusion(bf16[192,64,128]{2,0,1:T(8,128)(2,1)S(1)} %fusion.13, s32[1024]{0:T(1024)S(1)} %pad_clamp_fusion), kind=kCustom, calls=%fused_computation.1.clone | custom fusion | bytes 25166848 | tf_op jit(solution)/shard_map/jit(_take)/gather | solution.py:50
  101.4 0.0 copy-done.5
  101.4 14.6 %fusion = f32[256,128,128]{2,1,0:T(8,128)} fusion(bf16[256,192,128]{2,1,0:T(8,128)(2,1)} %gather_fusion.9, bf16[256,192,128]{2,1,0:T(8,128)(2,1)} %gather_fusion.8, pred[256]{0:T(512)(128)(4,1)S(1)} %get-tuple-element.7, pred[256]{0:T(512)(128)(4,1)S(1)} %get-tuple-element.8), kind=kOutput, calls=%fused_computation.10 | convolution fusion | flops 1623195648 | bytes 41943552 | tf_op jit(solution)/shard_map/rnc,rnd->ncd/dot_general | solution.py:52
  116.0 0.0 copy-start.2
  116.0 0.0 copy-start.3
  116.0 0.0 reduce-scatter.2.cloned.1.call-update
  116.0 0.0 all-reduce.2.cloned.1.call-start
  116.1 0.6 copy-done.2
  116.7 3.2 sort.31
  119.9 0.0 copy-done.3
  119.9 2.2 gather_fusion.4
  122.1 0.1 reshape.98
  122.2 0.1 reshape.159
  122.3 12.4 %gather_fusion.5 = bf16[256,192,128]{2,1,0:T(8,128)(2,1)} fusion(bf16[192,64,128]{2,0,1:T(8,128)(2,1)} %copy-done.5, s32[1024]{0:T(1024)S(1)} %pad_clamp_fusion.3), kind=kCustom, calls=%fused_computation.7 | custom fusion | bytes 25166848 | tf_op jit(solution)/shard_map/gather | solution.py:35
  134.7 12.2 %gather_fusion = bf16[256,128,128]{2,1,0:T(8,128)(2,1)} fusion(bf16[256,128,128]{2,1,0:T(8,128)(2,1)} %all-gather.2.cloned.1.call-done, s32[1024]{0:T(1024)S(1)} %pad_clamp_fusion.6), kind=kCustom, calls=%fused_computation.2 | custom fusion | bytes 16778240 | tf_op jit(solution)/shard_map/gather | solution.py:34
  146.9 155.1 %reduce-scatter.2.cloned.1.call-done = f32[16,128,128]{2,1,0:T(8,128)} async-done(((f32[256,128,128]{2,1,0:T(8,128)}), f32[16,128,128]{2,1,0:T(8,128)}) %reduce-scatter.2.cloned.1.call-update) | async-done | bytes 1048592 | tf_op jit(solution)/shard_map/reduce_scatter | solution.py:51
  301.9 0.0 all-reduce.2.cloned.1.call-update
  302.0 0.0 copy-start.1
  302.0 12.5 %fusion.18 = bf16[64,24,8,128]{3,2,1,0:T(8,128)(2,1)} fusion(bf16[64,4,128,128]{3,2,1,0:T(8,128)(2,1)} %bitcast.67, bf16[192,64,4,128]{3,0,2,1:T(8,128)(2,1)} %bitcast.66, bf16[192,8192]{1,0:T(8,128)(2,1)} %param.8), kind=kOutput, calls=%fused_computation.33 | convolution fusion | flops 1615331328 | bytes 27262976 | tf_op jit(solution)/shard_map/rnkd,nkcd->rnc/dot_general | solution.py:36
  314.5 4.4 copy.32
  319.0 153.1 %all-reduce.2.cloned.1.call-done = f32[16,128,128]{2,1,0:T(8,128)} async-done(((f32[16,128,128]{2,1,0:T(8,128)}), f32[16,128,128]{2,1,0:T(8,128)}) %all-reduce.2.cloned.1.call-update) | async-done | bytes 1048592 | tf_op jit(solution)/shard_map/psum | solution.py:57
  472.1 1.4 multiply_reduce_fusion
  473.5 2.3 broadcast_multiply_fusion
  475.9 0.0 copy-done.1
  (18 shorter events, 0.1 us)
Async XLA Ops:
  7.2 11.0 %copy-start = (bf16[192,8192]{1,0:T(8,128)(2,1)S(1)}, bf16[192,8192]{1,0:T(8,128)(2,1)}, u32[]{:S(2)}) copy-start(bf16[192,8192]{1,0:T(8,128)(2,1)} %param.7) | copy-start | bytes 9437188
  7.2 60.3 %all-gather.2.cloned.1.call-start = ((), (), s32[]{:S(2)}) async-start(), calls=%async_computation.1 | async-start | bytes 8912896 | tf_op jit(solution)/shard_map/all_gather | solution.py:29
  7.9 294.0 %reduce-scatter.2.cloned.1.call-start = ((), (), s32[]{:S(2)}) async-start(), calls=%async_computation.2 | async-start | bytes 17825792 | tf_op jit(solution)/shard_map/reduce_scatter | solution.py:51
  20.7 12.9 %copy-start.4 = (bf16[192,64,128]{2,0,1:T(8,128)(2,1)S(1)}, bf16[192,64,128]{2,0,1:T(8,128)(2,1)}, u32[]{:S(2)}) copy-start(bf16[192,64,128]{2,0,1:T(8,128)(2,1)} %copy_bitcast_fusion.1) | copy-start | bytes 9437188
  90.6 10.7 %copy-start.5 = (bf16[192,64,128]{2,0,1:T(8,128)(2,1)}, bf16[192,64,128]{2,0,1:T(8,128)(2,1)S(1)}, u32[]{:S(2)}) copy-start(bf16[192,64,128]{2,0,1:T(8,128)(2,1)S(1)} %fusion.13) | copy-start | bytes 9437188
  116.0 0.7 copy-start.2
  116.0 3.9 copy-start.3
  116.0 356.1 %all-reduce.2.cloned.1.call-start = ((), (), s32[]{:S(2)}) async-start(), calls=%async_computation.3 | async-start | bytes 2097152 | tf_op jit(solution)/shard_map/psum | solution.py:57
  302.0 173.9 %copy-start.1 = (bf16[192,8192]{1,0:T(8,128)(2,1)S(1)}, bf16[192,8192]{1,0:T(8,128)(2,1)}, u32[]{:S(2)}) copy-start(bf16[192,8192]{1,0:T(8,128)(2,1)} %param.7) | copy-start | bytes 9437188
Sparse Core Ops, SparseCore 0:
  9.9 57.6 all-gather.1
  116.2 185.7 reduce-scatter.1
  304.6 167.4 all-reduce.1
where the time goes:
time: 483 us; the launch traced here: 482 us
  waiting for transfers between devices  332 us (69%)
  local copies, waits for them, and re-layouts  87.2 us (18%)
  matrix products  38.2 us (8%)
  between operations  13.9 us (3%)
  other arithmetic  11 us (2%)
    reduce_scatter x1, waiting for transfers between devices, on_device(): lax.psum_scatter(jnp.einsum('rnc,rnd->ncd', picked, slopes, preferred_ele...  155 us
    psum x1, waiting for transfers between devices, on_device(): weight_grad = lax.psum(summed, 'dp')  153 us
    all_gather x1, waiting for transfers between devices, on_device(): whole = lax.all_gather(weight_tiles, 'fsdp', axis=0, tiled=True)  23.1 us
    dot_general x1, matrix products, on_device(): jnp.einsum('rnc,rnd->ncd', picked, slopes, preferred_element_type=jnp.flo...  14.6 us
    gather x1, local copies, waits for them, and re-layouts, on_device(): taken = feature_blocks[:, columns_by_row]  12.8 us
    dot_general x1, matrix products, on_device(): jnp.einsum('rnkd,nkcd->rnc', slopes_taken, tiles_by_column, preferred_ele...  12.5 us
    gather x1, local copies, waits for them, and re-layouts, on_device(): slopes_taken = slope_grad[:, rows_by_column]  12.4 us
    gather x1, local copies, waits for them, and re-layouts, on_device(): whole[order_columns].reshape(nblocks, per_block, side, side)  12.2 us
  transfers between devices with their start and end apart: 3, of which 3 were waited for; matrix products, arithmetic and copies ran while one was open for 17% of the time, Pallas kernels for 0%

commit v1 on v0

--- a/solution.py
+++ b/solution.py
@@ -26,7 +26,15 @@
     order_columns = jnp.argsort(tile_column, stable=True)
     columns_by_row = tile_column[order_rows].reshape(nblocks, per_block)
     rows_by_column = tile_row[order_columns].reshape(nblocks, per_block)
-    whole = lax.all_gather(weight_tiles, "fsdp", axis=0, tiled=True)
+    whole = jnp.concatenate(
+        lax.all_to_all(
+            jnp.stack([weight_tiles] * lax.axis_size("fsdp"), 0),
+            axis_name="fsdp",
+            split_axis=0,
+            concat_axis=0,
+        ),
+        0,
+    )
     tiles_by_row = whole[order_rows].reshape(nblocks, per_block, side, side)
     taken = feature_blocks[:, columns_by_row]
     preact = jnp.einsum("rnkc,nkcd->rnd", taken, tiles_by_row, preferred_element_type=jnp.float32)

time: 483 us -> 530 us (1.097)
  waiting for transfers between devices: 332 us -> 371 us
  starting transfers between devices: 0.12 us -> 6.02 us
    all_to_all x0 -> x1, waiting for transfers between devices: none -> 60.2 us  [on_device(): lax.all_to_all(jnp.stack([weight_tiles] * lax.axis_size('fsdp'), 0), axis...]
    all_gather x1 -> x0, waiting for transfers between devices: 23.1 us -> none  [on_device(): whole = lax.all_gather(weight_tiles, 'fsdp', axis=0, tiled=True)]
    another operation x0 -> x1, local copies, waits for them, and re-layouts: none -> 6.66 us  [on_device(): jnp.stack([weight_tiles] * lax.axis_size('fsdp'), 0)]
    all_to_all x0 -> x1, starting transfers between devices: none -> 5.94 us  [on_device(): lax.all_to_all(jnp.stack([weight_tiles] * lax.axis_size('fsdp'), 0), axis...]
  transfers between devices with their start and end apart: 3 -> 3, of which waited for: 3 -> 3; matrix products, arithmetic and copies ran while one was open for 17% -> 15% of each run, Pallas kernels for 0% -> 0%
where the time goes in v1:
time: 530 us
  waiting for transfers between devices  371 us (70%)
  local copies, waits for them, and re-layouts  90.5 us (17%)
  matrix products  38.2 us (7%)
  between operations  14.2 us (3%)
  other arithmetic  10.2 us (2%)
  starting transfers between devices  6.02 us (1%)
    reduce_scatter x1, waiting for transfers between devices, on_device(): lax.psum_scatter(jnp.einsum('rnc,rnd->ncd', picked, slopes, preferred_ele...  157 us
    psum x1, waiting for transfers between devices, on_device(): weight_grad = lax.psum(summed, 'dp')  153 us
    all_to_all x1, waiting for transfers between devices, on_device(): lax.all_to_all(jnp.stack([weight_tiles] * lax.axis_size('fsdp'), 0), axis...  60.2 us
    dot_general x1, matrix products, on_device(): jnp.einsum('rnc,rnd->ncd', picked, slopes, preferred_element_type=jnp.flo...  14.7 us
    dot_general x1, matrix products, on_device(): jnp.einsum('rnkd,nkcd->rnc', slopes_taken, tiles_by_column, preferred_ele...  12.5 us
    gather x1, local copies, waits for them, and re-layouts, on_device(): taken = feature_blocks[:, columns_by_row]  12.5 us
    gather x1, local copies, waits for them, and re-layouts, on_device(): whole[order_columns].reshape(nblocks, per_block, side, side)  12.1 us
    gather x1, local copies, waits for them, and re-layouts, on_device(): tiles_by_row = whole[order_rows].reshape(nblocks, per_block, side, side)  12.1 us
  transfers between devices with their start and end apart: 3, of which 3 were waited for; matrix products, arithmetic and copies ran while one was open for 15% of the time, Pallas kernels for 0%

profile of v1, /device:TPU:8, one launch (start us, length us, event | category | flops | bytes accessed | tf_op | source)
XLA Modules:
  0.0 529.9 jit_solution(12233217366795763389)
XLA Ops:
  7.2 0.0 copy-start
  7.2 6.7 %stack.2 = bf16[16,16,128,128]{3,2,1,0:T(8,128)(2,1)} broadcast(bf16[16,128,128]{2,1,0:T(8,128)(2,1)} %param.9), dimensions={1,2,3} | broadcast | bytes 8912896 | tf_op jit(solution)/shard_map/stack | solution.py:31
  13.8 0.0 copy-start.3
  13.8 0.0 copy-start.2
  13.8 5.9 %all-to-all-start = ((bf16[16,16,128,128]{3,2,1,0:T(8,128)(2,1)}), bf16[16,16,128,128]{3,2,1,0:T(8,128)(2,1)}, u32[]{:S(2)}, u32[]{:S(2)}) async-start(bf16[16,16,128,128]{3,2,1,0:T(8,128)(2,1)} %stack.2), calls=%async_computation | async-start | bytes 16777216 | tf_op jit(solution)/shard_map/all_to_all | solution.py:30
  19.8 0.0 reduce-scatter.2.cloned.1.call-start
  19.9 0.0 copy-done.3
  19.9 3.2 sort.32
  23.0 1.9 gather_fusion.7
  25.0 0.0 copy-done.2
  25.0 1.9 gather_fusion.6
  27.0 1.9 gather_fusion.2
  28.9 0.1 reshape.103
  29.0 0.1 reshape.149
  29.2 0.0 copy-done
  29.2 2.6 copy_bitcast_fusion.1
  31.7 0.0 copy-start.4
  31.7 12.5 %gather_fusion.3 = bf16[256,192,128]{2,1,0:T(8,128)(2,1)} fusion(bf16[192,64,128]{2,0,1:T(8,128)(2,1)} %copy_bitcast_fusion.1, s32[1024]{0:T(1024)S(1)} %pad_clamp_fusion.4), kind=kCustom, calls=%fused_computation.5 | custom fusion | bytes 25166848 | tf_op jit(solution)/shard_map/gather | solution.py:39
  44.3 0.0 copy-done.4
  44.3 10.6 %gather_fusion.8 = bf16[256,192,128]{2,1,0:T(8,128)(2,1)} fusion(bf16[192,64,128]{2,0,1:T(8,128)(2,1)S(1)} %copy-done.4, s32[1024]{0:T(1024)S(1)} %pad_clamp_fusion.1), kind=kCustom, calls=%fused_computation.clone | custom fusion | bytes 25166848 | tf_op jit(solution)/shard_map/jit(_take)/gather | solution.py:57
  54.9 60.2 %all-to-all-done = bf16[16,16,128,128]{3,2,1,0:T(8,128)(2,1)} async-done(((bf16[16,16,128,128]{3,2,1,0:T(8,128)(2,1)}), bf16[16,16,128,128]{3,2,1,0:T(8,128)(2,1)}, u32[]{:S(2)}, u32[]{:S(2)}) %all-to-all-start) | async-done | bytes 8388640 | tf_op jit(solution)/shard_map/all_to_all | solution.py:30
  115.1 12.1 %gather_fusion.1 = bf16[256,128,128]{2,1,0:T(8,128)(2,1)} fusion(bf16[256,128,128]{2,1,0:T(8,128)(2,1)} %bitcast, s32[1024]{0:T(1024)S(1)} %pad_clamp_fusion.5), kind=kCustom, calls=%fused_computation.3 | custom fusion | bytes 16778240 | tf_op jit(solution)/shard_map/gather | solution.py:38
  127.2 11.0 %fusion.13 = bf16[192,64,128]{2,0,1:T(8,128)(2,1)S(1)} fusion(bf16[192,64,4,128]{3,0,2,1:T(8,128)(2,1)} %bitcast.66, bf16[64,4,128,128]{3,2,1,0:T(8,128)(2,1)} %bitcast.69, bf16[192,8192]{1,0:T(8,128)(2,1)} %param.8), kind=kOutput, calls=%fused_computation.25 | convolution fusion | flops 1642070016 | bytes 27262976 | tf_op jit(solution)/shard_map/rnkc,nkcd->rnd/dot_general | solution.py:40
  138.2 10.5 %gather_fusion.9 = bf16[256,192,128]{2,1,0:T(8,128)(2,1)} fusion(bf16[192,64,128]{2,0,1:T(8,128)(2,1)S(1)} %fusion.13, s32[1024]{0:T(1024)S(1)} %pad_clamp_fusion), kind=kCustom, calls=%fused_computation.1.clone | custom fusion | bytes 25166848 | tf_op jit(solution)/shard_map/jit(_take)/gather | solution.py:58
  148.7 14.7 %fusion = f32[256,128,128]{2,1,0:T(8,128)} fusion(bf16[256,192,128]{2,1,0:T(8,128)(2,1)} %gather_fusion.9, bf16[256,192,128]{2,1,0:T(8,128)(2,1)} %gather_fusion.8, pred[256]{0:T(512)(128)(4,1)S(1)} %get-tuple-element.7, pred[256]{0:T(512)(128)(4,1)S(1)} %get-tuple-element.8), kind=kOutput, calls=%fused_computation.10 | convolution fusion | flops 1623195648 | bytes 41943552 | tf_op jit(solution)/shard_map/rnc,rnd->ncd/dot_general | solution.py:60
  163.4 0.0 reduce-scatter.2.cloned.1.call-update
  163.4 0.0 all-reduce.2.cloned.1.call-start
  163.5 3.2 sort.31
  166.7 2.2 gather_fusion.4
  168.9 0.1 reshape.104
  169.0 0.1 reshape.165
  169.1 12.1 %gather_fusion = bf16[256,128,128]{2,1,0:T(8,128)(2,1)} fusion(bf16[256,128,128]{2,1,0:T(8,128)(2,1)} %bitcast, s32[1024]{0:T(1024)S(1)} %pad_clamp_fusion.6), kind=kCustom, calls=%fused_computation.2 | custom fusion | bytes 16778240 | tf_op jit(solution)/shard_map/gather | solution.py:42
  181.2 10.5 %gather_fusion.5 = bf16[256,192,128]{2,1,0:T(8,128)(2,1)} fusion(bf16[192,64,128]{2,0,1:T(8,128)(2,1)S(1)} %fusion.13, s32[1024]{0:T(1024)S(1)} %pad_clamp_fusion.3), kind=kCustom, calls=%fused_computation.7 | custom fusion | bytes 25166848 | tf_op jit(solution)/shard_map/gather | solution.py:43
  191.8 157.3 %reduce-scatter.2.cloned.1.call-done = f32[16,128,128]{2,1,0:T(8,128)} async-done(((f32[256,128,128]{2,1,0:T(8,128)}), f32[16,128,128]{2,1,0:T(8,128)}) %reduce-scatter.2.cloned.1.call-update) | async-done | bytes 1048592 | tf_op jit(solution)/shard_map/reduce_scatter | solution.py:59
  349.1 0.0 all-reduce.2.cloned.1.call-update
  349.1 0.0 copy-start.1
  349.1 12.5 %fusion.18 = bf16[64,24,8,128]{3,2,1,0:T(8,128)(2,1)} fusion(bf16[64,4,128,128]{3,2,1,0:T(8,128)(2,1)} %bitcast.68, bf16[192,64,4,128]{3,0,2,1:T(8,128)(2,1)} %bitcast.67, bf16[192,8192]{1,0:T(8,128)(2,1)} %param.8), kind=kOutput, calls=%fused_computation.33 | convolution fusion | flops 1615331328 | bytes 27262976 | tf_op jit(solution)/shard_map/rnkd,nkcd->rnc/dot_general | solution.py:44
  361.6 4.4 copy.27
  366.1 153.2 %all-reduce.2.cloned.1.call-done = f32[16,128,128]{2,1,0:T(8,128)} async-done(((f32[16,128,128]{2,1,0:T(8,128)}), f32[16,128,128]{2,1,0:T(8,128)}) %all-reduce.2.cloned.1.call-update) | async-done | bytes 1048592 | tf_op jit(solution)/shard_map/psum | solution.py:65
  519.2 1.4 multiply_reduce_fusion
  520.7 2.3 broadcast_multiply_fusion
  523.0 0.0 copy-done.1
  (18 shorter events, 0.1 us)
Async XLA Ops:
  7.2 22.0 %copy-start = (bf16[192,8192]{1,0:T(8,128)(2,1)S(1)}, bf16[192,8192]{1,0:T(8,128)(2,1)}, u32[]{:S(2)}) copy-start(bf16[192,8192]{1,0:T(8,128)(2,1)} %param.7) | copy-start | bytes 9437188
  13.8 6.0 %copy-start.3 = (s32[256]{0:T(256)S(1)}, s32[256]{0:T(256)}, u32[]{:S(2)}) copy-start(s32[256]{0:T(256)} %param.10) | copy-start | bytes 3076
  13.8 11.1 %copy-start.2 = (s32[256]{0:T(256)S(1)}, s32[256]{0:T(256)}, u32[]{:S(2)}) copy-start(s32[256]{0:T(256)} %param.11) | copy-start | bytes 3076
  13.8 101.3 %all-to-all-start = ((bf16[16,16,128,128]{3,2,1,0:T(8,128)(2,1)}), bf16[16,16,128,128]{3,2,1,0:T(8,128)(2,1)}, u32[]{:S(2)}, u32[]{:S(2)}) async-start(bf16[16,16,128,128]{3,2,1,0:T(8,128)(2,1)} %stack.2), calls=%async_computation | async-start | bytes 16777216 | tf_op jit(solution)/shard_map/all_to_all | solution.py:30
  19.8 329.3 %reduce-scatter.2.cloned.1.call-start = ((), (), s32[]{:S(2)}) async-start(), calls=%async_computation.2 | async-start | bytes 17825792 | tf_op jit(solution)/shard_map/reduce_scatter | solution.py:59
  31.7 12.5 %copy-start.4 = (bf16[192,64,128]{2,0,1:T(8,128)(2,1)S(1)}, bf16[192,64,128]{2,0,1:T(8,128)(2,1)}, u32[]{:S(2)}) copy-start(bf16[192,64,128]{2,0,1:T(8,128)(2,1)} %copy_bitcast_fusion.1) | copy-start | bytes 9437188
  163.4 355.8 %all-reduce.2.cloned.1.call-start = ((), (), s32[]{:S(2)}) async-start(), calls=%async_computation.3 | async-start | bytes 2097152 | tf_op jit(solution)/shard_map/psum | solution.py:65
  349.1 173.9 %copy-start.1 = (bf16[192,8192]{1,0:T(8,128)(2,1)S(1)}, bf16[192,8192]{1,0:T(8,128)(2,1)}, u32[]{:S(2)}) copy-start(bf16[192,8192]{1,0:T(8,128)(2,1)} %param.7) | copy-start | bytes 9437188
Sparse Core Ops, SparseCore 0:
  163.6 185.4 reduce-scatter.1
  351.7 167.5 all-reduce.1
